TPU v7x, 32 devices: a whole 2x2x4 slice. The times are simulated.
32 devices in a mesh: dp: 4 (over x, core), blk: 8 (over z, y).
Axes of the slice: x: 2, y: 2, z: 4, core: 2. Of those that a mesh axis runs over, the one named last changes fastest.
Arguments:
- hidden_in: bfloat16 [2048, 8, 1024], P('blk', 'dp'), may hold values from -6 to 6
- first_values: bfloat16 [2048, 8, 1024], P('blk', 'dp'), may hold values from -13 to 13
- doc_lengths: int32 [8, 8], P('dp'), may hold values from 1 to 1024, 2048 in all within a row
- w_query: bfloat16 [1024, 1024], replicated, may hold values from -0.25 to 0.25
- w_key: bfloat16 [1024, 1024], replicated, may hold values from -0.25 to 0.25
- w_value: bfloat16 [1024, 1024], replicated, may hold values from -0.1875 to 0.1875
- w_out: bfloat16 [1024, 1024], replicated, may hold values from -0.75 to 0.75
- w_gate: bfloat16 [1024, 2816], replicated, may hold values from -0.1875 to 0.1875
- w_up: bfloat16 [1024, 2816], replicated, may hold values from -0.1875 to 0.1875
- w_down: bfloat16 [2816, 1024], replicated, may hold values from -0.109375 to 0.109375
- attn_gain: float32 [1024], replicated, may hold values from 0.5 to 1.5
- ffn_gain: float32 [1024], replicated, may hold values from 0.5 to 1.5
- out_cotangent: bfloat16 [2048, 8, 1024], P('blk', 'dp'), may hold values from -6 to 6
Outputs:
- block_out: bfloat16 [2048, 8, 1024], P('blk', 'dp')
- grad_input: float32 [2048, 8, 1024], P('blk', 'dp')
- grad_first: float32 [2048, 8, 1024], P('blk', 'dp')
- grad_query: float32 [1024, 1024], P('dp', 'blk')
- grad_key: float32 [1024, 1024], P('dp', 'blk')
- grad_value: float32 [1024, 1024], P('dp', 'blk')
- grad_project: float32 [1024, 1024], P('dp', 'blk')
- grad_gate: float32 [1024, 2816], P('dp', 'blk')
- grad_up: float32 [1024, 2816], P('dp', 'blk')
- grad_down: float32 [2816, 1024], P('dp', 'blk')
- grad_attn_gain: float32 [1024], replicated
- grad_ffn_gain: float32 [1024], replicated
- first_msq: float32 [], replicated
- mixed_msq: float32 [], replicated
Inputs may be any that keep to these rules, and one draw needn't show every extreme that they name: `doc_lengths`: the 8 lengths of a row sum to 2048.
All inputs are finite; a program needn't handle non-finite values.
Results may differ from a plain program's by a relative error of at most 0.033.
Values may be sent and summed in bfloat16 or wider, within the bound.
A program may use at most 320 MiB of HBM per device.

v0:
```python
import jax
import jax.numpy as jnp
from jax import lax
from jax.sharding import PartitionSpec as P

HEADS = 16
HEAD_DIM = 64
epsilon = 1e-06


def documents(doc_lengths, row_length):
    doc_ends = jnp.cumsum(doc_lengths, axis=1)
    places = jnp.arange(row_length, dtype=jnp.int32)
    passed = (doc_ends[:, None, :] <= places[None, :, None]).astype(jnp.int32)
    segment = jnp.sum(passed, axis=2)
    doc_start = jnp.sum(passed * doc_lengths[:, None, :], axis=2)
    return (segment, places[None, :] - doc_start)


def project(acts, weight):
    flat = acts.reshape(-1, acts.shape[-1])
    result = jnp.dot(flat, weight, preferred_element_type=jnp.float32)
    return result.reshape(acts.shape[:-1] + (weight.shape[1],))


def project_back(grads_in, weight):
    flat = grads_in.reshape(-1, grads_in.shape[-1])
    result = lax.dot_general(
        flat, weight, (((1,), (1,)), ((), ())), preferred_element_type=jnp.float32
    )
    return result.reshape(grads_in.shape[:-1] + (weight.shape[0],))


def weight_grad(acts, grads_in):
    flat_acts = acts.reshape(-1, acts.shape[-1])
    flat_grads = grads_in.reshape(-1, grads_in.shape[-1])
    return lax.dot_general(
        flat_acts, flat_grads, (((0,), (0,)), ((), ())), preferred_element_type=jnp.float32
    )


def rms_parts(values):
    inverse_rms = lax.rsqrt(jnp.mean(values * values, axis=-1, keepdims=True) + epsilon)
    return (values * inverse_rms, inverse_rms)


def norm_back(d_normed, normed, inverse_rms):
    return inverse_rms * (d_normed - normed * jnp.mean(d_normed * normed, axis=-1, keepdims=True))


def rope_tables(positions):
    half_dim = HEAD_DIM // 2
    inverse_freq = jnp.power(10000.0, -jnp.arange(half_dim, dtype=jnp.float32) * 2.0 / HEAD_DIM)
    angles = jnp.transpose(positions).astype(jnp.float32)[:, :, None] * inverse_freq[None, None, :]
    return (jnp.cos(angles)[:, :, None, :], jnp.sin(angles)[:, :, None, :])


def rotate(values, cos_table, sin_table):
    half_dim = HEAD_DIM // 2
    shaped = values.reshape(values.shape[:-1] + (HEADS, HEAD_DIM))
    first_half = shaped[..., :half_dim]
    second_half = shaped[..., half_dim:]
    turned = jnp.concatenate(
        [
            first_half * cos_table - second_half * sin_table,
            second_half * cos_table + first_half * sin_table,
        ],
        axis=-1,
    )
    return turned.reshape(values.shape)


def body(
    hidden_in,
    first_values,
    doc_lengths,
    w_query,
    w_key,
    w_value,
    w_out,
    w_gate,
    w_up,
    w_down,
    attn_gain,
    ffn_gain,
    out_cotangent,
):
    local_len, seq_count, model_width = hidden_in.shape
    cycle_size = lax.axis_size("blk")
    row_length = local_len * cycle_size
    offset = lax.axis_index("blk") * local_len
    score_scale = HEAD_DIM ** (-0.5)
    segment_all, position_all = documents(doc_lengths, row_length)
    segment_own = lax.dynamic_slice_in_dim(segment_all, offset, local_len, 1)
    position_own = lax.dynamic_slice_in_dim(position_all, offset, local_len, 1)
    query_index = offset + jnp.arange(local_len, dtype=jnp.int32)
    cos_table, sin_table = rope_tables(position_own)
    resid_in = hidden_in.astype(jnp.float32)
    normed_one, inv_one = rms_parts(resid_in)
    normed_in = (normed_one * attn_gain).astype(jnp.bfloat16)
    queries = rotate(project(normed_in, w_query), cos_table, sin_table).astype(jnp.bfloat16)
    keys_rot = rotate(project(normed_in, w_key), cos_table, sin_table).astype(jnp.bfloat16)
    first_f = first_values.astype(jnp.float32)
    mixed = 0.5 * project(normed_in, w_value) + 0.5 * first_f
    mixed_low = mixed.astype(jnp.bfloat16)
    first_sq = jnp.sum(first_f * first_f)
    mixed_sq = jnp.sum(mixed * mixed)
    query_four = queries.reshape(local_len, seq_count, HEADS, HEAD_DIM)

    def allowed_pairs(start, n_keys):
        key_index = start + jnp.arange(n_keys, dtype=jnp.int32)
        segment_key = lax.dynamic_slice_in_dim(segment_all, start, n_keys, 1)
        allowed = (key_index[None, None, :] <= query_index[None, :, None]) & (
            segment_key[:, None, :] == segment_own[:, :, None]
        )
        return allowed[:, None]

    def piece_step(running, key_piece, value_piece, start):
        run_max, run_sum, run_acc = running
        n_keys = key_piece.shape[0]
        allowed = allowed_pairs(start, n_keys)
        key_four = key_piece.reshape(n_keys, seq_count, HEADS, HEAD_DIM)
        value_four = value_piece.reshape(n_keys, seq_count, HEADS, HEAD_DIM)
        scores = (
            jnp.einsum("qshd,kshd->shqk", query_four, key_four, preferred_element_type=jnp.float32)
            * score_scale
        )
        new_max = jnp.maximum(run_max, jnp.max(jnp.where(allowed, scores, -1e30), axis=-1))
        weights = jnp.where(allowed, jnp.exp(scores - new_max[..., None]), 0.0)
        factor = jnp.exp(run_max - new_max)
        run_sum = run_sum * factor + jnp.sum(weights, axis=-1)
        run_acc = run_acc * factor[..., None] + jnp.einsum(
            "shqk,kshd->shqd",
            weights.astype(jnp.bfloat16),
            value_four,
            preferred_element_type=jnp.float32,
        )
        return (new_max, run_sum, run_acc)

    start_state = (
        jnp.full((seq_count, HEADS, local_len), -1e30, jnp.float32),
        jnp.zeros((seq_count, HEADS, local_len), jnp.float32),
        jnp.zeros((seq_count, HEADS, local_len, HEAD_DIM), jnp.float32),
    )
    running = start_state
    key_piece = lax.all_gather(keys_rot, "blk", axis=0, tiled=True)
    value_piece = lax.all_gather(mixed_low, "blk", axis=0, tiled=True)
    n_keys = key_piece.shape[0]
    step_rows = min(512, n_keys)
    n_steps = n_keys // step_rows

    def inner_step(fold_state, block_item):
        return (piece_step(fold_state, block_item[0], block_item[1], block_item[2]), None)

    starts = jnp.arange(n_steps, dtype=jnp.int32) * step_rows
    running, unused = lax.scan(
        inner_step,
        running,
        (
            key_piece.reshape(n_steps, step_rows, seq_count, model_width),
            value_piece.reshape(n_steps, step_rows, seq_count, model_width),
            starts,
        ),
    )
    run_max, run_sum, run_acc = running
    attn_four = jnp.transpose(run_acc / run_sum[..., None], (2, 0, 1, 3))
    attn_f = attn_four.reshape(local_len, seq_count, model_width)
    log_total = run_max + jnp.log(run_sum)
    attn_low = attn_f.astype(jnp.bfloat16)
    resid_mid = resid_in + project(attn_low, w_out)
    normed_two, inv_two = rms_parts(resid_mid)
    normed_mid = (normed_two * ffn_gain).astype(jnp.bfloat16)
    gate_pre = project(normed_mid, w_gate)
    up_pre = project(normed_mid, w_up)
    gate_act = jax.nn.silu(gate_pre)
    inner_low = (gate_act * up_pre).astype(jnp.bfloat16)
    block_out = (resid_mid + project(inner_low, w_down)).astype(jnp.bfloat16)
    grad_down = weight_grad(inner_low, out_cotangent)
    d_inner = project_back(out_cotangent, w_down)
    sigmoid_gate = jax.nn.sigmoid(gate_pre)
    d_gate = (d_inner * up_pre * sigmoid_gate * (1.0 + gate_pre * (1.0 - sigmoid_gate))).astype(
        jnp.bfloat16
    )
    d_up = (d_inner * gate_act).astype(jnp.bfloat16)
    grad_gate = weight_grad(normed_mid, d_gate)
    grad_up = weight_grad(normed_mid, d_up)
    d_normed_mid = project_back(d_gate, w_gate) + project_back(d_up, w_up)
    gain_two_grad = jnp.sum((d_normed_mid * normed_two).reshape(-1, model_width), axis=0)
    d_resid_mid = out_cotangent.astype(jnp.float32) + norm_back(
        d_normed_mid * ffn_gain, normed_two, inv_two
    )
    d_branch = d_resid_mid.astype(jnp.bfloat16)
    grad_project = weight_grad(attn_low, d_branch)
    d_attn = project_back(d_branch, w_out).astype(jnp.bfloat16)
    d_attn_four = d_attn.reshape(local_len, seq_count, HEADS, HEAD_DIM)
    delta_rows = jnp.transpose(
        jnp.sum(d_attn_four.astype(jnp.float32) * attn_four, axis=-1), (1, 2, 0)
    )
    back_keys, back_values = (
        lax.all_gather(keys_rot, "blk", axis=0, tiled=True),
        lax.all_gather(mixed_low, "blk", axis=0, tiled=True),
    )
    block_rows = min(512, row_length)
    n_blocks = row_length // block_rows
    block_starts = jnp.arange(n_blocks, dtype=jnp.int32) * block_rows

    def block_scores(key_four, value_four, start):
        allowed = allowed_pairs(start, block_rows)
        scores = (
            jnp.einsum("qshd,kshd->shqk", query_four, key_four, preferred_element_type=jnp.float32)
            * score_scale
        )
        probs = jnp.where(allowed, jnp.exp(scores - log_total[..., None]), 0.0)
        d_probs = jnp.einsum(
            "qshd,kshd->shqk", d_attn_four, value_four, preferred_element_type=jnp.float32
        )
        d_scores = (probs * (d_probs - delta_rows[..., None])).astype(jnp.bfloat16)
        return (probs, d_scores)

    def back_step(d_query_acc, block_item):
        key_block, value_block, start = block_item
        key_four = key_block.reshape(block_rows, seq_count, HEADS, HEAD_DIM)
        value_four = value_block.reshape(block_rows, seq_count, HEADS, HEAD_DIM)
        probs, d_scores = block_scores(key_four, value_four, start)
        d_query_acc = (
            d_query_acc
            + jnp.einsum("shqk,kshd->qshd", d_scores, key_four, preferred_element_type=jnp.float32)
            * score_scale
        )
        d_keys = (
            jnp.einsum("shqk,qshd->kshd", d_scores, query_four, preferred_element_type=jnp.float32)
            * score_scale
        )
        d_vals = jnp.einsum(
            "shqk,qshd->kshd",
            probs.astype(jnp.bfloat16),
            d_attn_four,
            preferred_element_type=jnp.float32,
        )
        joined = jnp.concatenate(
            [
                d_keys.reshape(block_rows, seq_count, model_width),
                d_vals.reshape(block_rows, seq_count, model_width),
            ],
            axis=-1,
        )
        return (d_query_acc, joined)

    d_query_rot, terms = lax.scan(
        back_step,
        jnp.zeros((local_len, seq_count, HEADS, HEAD_DIM), jnp.float32),
        (
            back_keys.reshape(n_blocks, block_rows, seq_count, model_width),
            back_values.reshape(n_blocks, block_rows, seq_count, model_width),
            block_starts,
        ),
    )
    terms = terms.reshape(row_length, seq_count, 2 * model_width)
    kv_grad = lax.psum_scatter(
        terms.astype(jnp.bfloat16), "blk", scatter_dimension=0, tiled=True
    ).astype(jnp.float32)
    d_key_rot = kv_grad[..., :model_width]
    d_mixed = kv_grad[..., model_width:]
    d_query_low = rotate(
        d_query_rot.reshape(local_len, seq_count, model_width), cos_table, -sin_table
    ).astype(jnp.bfloat16)
    d_key_low = rotate(d_key_rot, cos_table, -sin_table).astype(jnp.bfloat16)
    d_value_low = (0.5 * d_mixed).astype(jnp.bfloat16)
    grad_first = 0.5 * d_mixed
    grad_query = weight_grad(normed_in, d_query_low)
    grad_key = weight_grad(normed_in, d_key_low)
    grad_value = weight_grad(normed_in, d_value_low)
    d_normed_in = (
        project_back(d_query_low, w_query)
        + project_back(d_key_low, w_key)
        + project_back(d_value_low, w_value)
    )
    gain_one_grad = jnp.sum((d_normed_in * normed_one).reshape(-1, model_width), axis=0)
    grad_input = d_resid_mid + norm_back(d_normed_in * attn_gain, normed_one, inv_one)
    weight_grads = (grad_query, grad_key, grad_value, grad_project, grad_gate, grad_up, grad_down)
    partial_grads = (
        lax.psum_scatter(
            weight_grads[0].astype(jnp.bfloat16), "dp", scatter_dimension=0, tiled=True
        ).astype(jnp.float32),
        lax.psum_scatter(
            weight_grads[1].astype(jnp.bfloat16), "dp", scatter_dimension=0, tiled=True
        ).astype(jnp.float32),
        lax.psum_scatter(
            weight_grads[2].astype(jnp.bfloat16), "dp", scatter_dimension=0, tiled=True
        ).astype(jnp.float32),
        lax.psum_scatter(
            weight_grads[3].astype(jnp.bfloat16), "dp", scatter_dimension=0, tiled=True
        ).astype(jnp.float32),
        lax.psum_scatter(
            weight_grads[4].astype(jnp.bfloat16), "dp", scatter_dimension=0, tiled=True
        ).astype(jnp.float32),
        lax.psum_scatter(
            weight_grads[5].astype(jnp.bfloat16), "dp", scatter_dimension=0, tiled=True
        ).astype(jnp.float32),
        lax.psum_scatter(
            weight_grads[6].astype(jnp.bfloat16), "dp", scatter_dimension=0, tiled=True
        ).astype(jnp.float32),
    )
    summed = (
        lax.psum_scatter(
            partial_grads[0].astype(jnp.bfloat16), "blk", scatter_dimension=1, tiled=True
        ).astype(jnp.float32),
        lax.psum_scatter(
            partial_grads[1].astype(jnp.bfloat16), "blk", scatter_dimension=1, tiled=True
        ).astype(jnp.float32),
        lax.psum_scatter(
            partial_grads[2].astype(jnp.bfloat16), "blk", scatter_dimension=1, tiled=True
        ).astype(jnp.float32),
        lax.psum_scatter(
            partial_grads[3].astype(jnp.bfloat16), "blk", scatter_dimension=1, tiled=True
        ).astype(jnp.float32),
        lax.psum_scatter(
            partial_grads[4].astype(jnp.bfloat16), "blk", scatter_dimension=1, tiled=True
        ).astype(jnp.float32),
        lax.psum_scatter(
            partial_grads[5].astype(jnp.bfloat16), "blk", scatter_dimension=1, tiled=True
        ).astype(jnp.float32),
        lax.psum_scatter(
            partial_grads[6].astype(jnp.bfloat16), "blk", scatter_dimension=1, tiled=True
        ).astype(jnp.float32),
    )
    totals = lax.psum((gain_one_grad, gain_two_grad, first_sq, mixed_sq), ("dp", "blk"))
    n_entries = row_length * seq_count * lax.axis_size("dp") * model_width
    return (
        block_out,
        grad_input,
        grad_first,
        summed[0],
        summed[1],
        summed[2],
        summed[3],
        summed[4],
        summed[5],
        summed[6],
        totals[0],
        totals[1],
        totals[2] / n_entries,
        totals[3] / n_entries,
    )


def solution(mesh):
    in_specs = (
        P("blk", "dp", None),
        P("blk", "dp", None),
        P("dp", None),
        P(),
        P(),
        P(),
        P(),
        P(),
        P(),
        P(),
        P(),
        P(),
        P("blk", "dp", None),
    )
    out_specs = (
        P("blk", "dp", None),
        P("blk", "dp", None),
        P("blk", "dp", None),
        P("dp", "blk"),
        P("dp", "blk"),
        P("dp", "blk"),
        P("dp", "blk"),
        P("dp", "blk"),
        P("dp", "blk"),
        P("dp", "blk"),
        P(),
        P(),
        P(),
        P(),
    )
    return jax.shard_map(body, mesh=mesh, in_specs=in_specs, out_specs=out_specs, check_vma=False)
```

profile of v0, /device:TPU:0, one launch (start us, length us, event | category | flops | bytes accessed | tf_op | source)
XLA Modules:
  0.0 1740.5 jit_solution(13050748668814698923)
XLA Ops:
  34.5 7.7 fusion.29
  42.2 99.5 %all-gather.5.cloned.1.call-done = bf16[2048,2,1024]{2,0,1:T(8,128)(2,1)} async-done(((bf16[256,2,1024]{2,0,1:T(8,128)(2,1)}), bf16[2048,2,1024]{2,0,1:T(8,128)(2,1)}) %all-gather.5.cloned.1.call-update) | async-done | bytes 8388624 | tf_op jit(solution)/shard_map/all_gather | solution.py:147
  141.7 11.7 copy.140
  153.4 114.2 %all-gather.3.cloned.1.call-done = bf16[2048,2,1024]{2,0,1:T(8,128)(2,1)} async-done(((bf16[256,2,1024]{2,0,1:T(8,128)(2,1)}), bf16[2048,2,1024]{2,0,1:T(8,128)(2,1)}) %all-gather.3.cloned.1.call-update) | async-done | bytes 8388624 | tf_op jit(solution)/shard_map/all_gather | solution.py:146
  267.6 11.5 copy.139
  279.1 144.7 %while.28 = (s32[]{:T(128)}, f32[2,16,256]{2,1,0:T(8,128)S(1)}, f32[2,16,256]{2,1,0:T(8,128)S(1)}, f32[2,16,256,64]{2,3,1,0:T(8,128)}, s32[4]{0:T(128)S(1)}, /*i...) while((s32[]{:T(128)}, f32[2,16,256]{2,1,0:T(8,128)S(1)}, ...), condition=%wide.region_7.8_spmd.clone, body=%wide.region_4.0_spmd.clone.sunk | while | flops 1122149120 | bytes 70013144 | solution.py:156
  294.6 9.2 fusion.159
  303.7 11.1 fusion.161
  330.2 9.2 fusion.159
  339.4 11.7 fusion.161
  359.3 7.2 fusion.158
  366.5 9.2 fusion.159
  375.7 11.7 fusion.161
  402.8 9.2 fusion.159
  412.0 11.7 fusion.161
  428.1 8.4 fusion.35
  436.6 10.4 multiply_convert_fusion.1
  465.8 192.9 %while.29 = (s32[]{:T(128)}, f32[256,2,16,64]{0,3,2,1:T(8,128)}, bf16[4,512,2,2048]{1,3,2,0:T(8,128)(2,1)}, bf16[4,512,2,1024]{1,3,2,0:T(8,128)(2,1)}, s32[4]{0:...) while((s32[]{:T(128)}, f32[256,2,16,64]{0,3,2,1:T(8,128)}, ...), condition=%wide.region_12.13_spmd.clone, body=%wide.region_11.12_spmd.clone.sunk | while | flops 2739012352 | bytes 129093912 | solution.py:249
  475.5 8.2 fusion.172
  483.7 10.6 fusion.174
  494.2 9.4 fusion.173
  522.6 8.1 fusion.172
  530.7 10.6 fusion.174
  541.3 9.4 fusion.173
  571.2 8.1 fusion.172
  579.3 10.6 fusion.174
  589.9 9.4 fusion.173
  619.7 8.1 fusion.172
  627.8 10.6 fusion.174
  638.4 9.4 fusion.173
  658.7 21.6 %copy.148 = bf16[4,512,2,2048]{3,1,0,2:T(8,128)(2,1)} copy(bf16[4,512,2,2048]{1,3,2,0:T(8,128)(2,1)} %get-tuple-element.145) | data formatting | bytes 33554432 | tf_op jit(solution)/shard_map/convert_element_type | solution.py:260
  709.0 251.6 %reduce-scatter.30.cloned.1.call-done = bf16[256,2,2048]{2,0,1:T(8,128)(2,1)} async-done(((bf16[2048,2,2048]{2,0,1:T(8,128)(2,1)}), bf16[256,2,2048]{2,0,1:T(8,128)(2,1)}) %reduce-scatter.30.cloned.1.call-update) | async-done | bytes 2097168 | tf_op jit(solution)/shard_map/reduce_scatter | solution.py:259
  967.9 26.4 %reduce-scatter.38.cloned.1.call-done = bf16[256,1024]{1,0:T(8,128)(2,1)} async-done(((bf16[1024,1024]{1,0:T(8,128)(2,1)}), bf16[256,1024]{1,0:T(8,128)(2,1)}) %reduce-scatter.38.cloned.1.call-update) | async-done | bytes 524304 | tf_op jit(solution)/shard_map/reduce_scatter | solution.py:291
  996.4 55.2 %reduce-scatter.40.cloned.1.call-done = bf16[256,2816]{1,0:T(8,128)(2,1)} async-done(((bf16[1024,2816]{1,0:T(8,128)(2,1)}), bf16[256,2816]{1,0:T(8,128)(2,1)}) %reduce-scatter.40.cloned.1.call-update) | async-done | bytes 1441808 | tf_op jit(solution)/shard_map/reduce_scatter | solution.py:294
  1054.2 54.8 %reduce-scatter.42.cloned.1.call-done = bf16[256,2816]{1,0:T(8,128)(2,1)} async-done(((bf16[1024,2816]{1,0:T(8,128)(2,1)}), bf16[256,2816]{1,0:T(8,128)(2,1)}) %reduce-scatter.42.cloned.1.call-update) | async-done | bytes 1441808 | tf_op jit(solution)/shard_map/reduce_scatter | solution.py:297
  1111.7 54.8 %reduce-scatter.44.cloned.1.call-done = bf16[704,1024]{1,0:T(8,128)(2,1)} async-done(((bf16[2816,1024]{1,0:T(8,128)(2,1)}), bf16[704,1024]{1,0:T(8,128)(2,1)}) %reduce-scatter.44.cloned.1.call-update) | async-done | bytes 1441808 | tf_op jit(solution)/shard_map/reduce_scatter | solution.py:300
  1187.5 13.2 reduce-scatter.36.cloned.1.call-done
  1205.1 7.2 add_convert_fusion
  1214.4 51.5 %reduce-scatter.52.cloned.1.call-done = bf16[128,256]{1,0:T(8,128)(2,1)} async-done(((bf16[1024,256]{1,0:T(8,128)(2,1)}), bf16[128,256]{1,0:T(8,128)(2,1)}) %reduce-scatter.52.cloned.1.call-update) | async-done | bytes 65552
  1267.6 66.0 %reduce-scatter.54.cloned.1.call-done = bf16[352,256]{1,0:T(8,128)(2,1)} async-done(((bf16[2816,256]{1,0:T(8,128)(2,1)}), bf16[352,256]{1,0:T(8,128)(2,1)}) %reduce-scatter.54.cloned.1.call-update) | async-done | bytes 180240
  1335.5 65.7 %reduce-scatter.56.cloned.1.call-done = bf16[352,256]{1,0:T(8,128)(2,1)} async-done(((bf16[2816,256]{1,0:T(8,128)(2,1)}), bf16[352,256]{1,0:T(8,128)(2,1)}) %reduce-scatter.56.cloned.1.call-update) | async-done | bytes 180240
  1403.2 65.4 %reduce-scatter.58.cloned.1.call-done = bf16[128,704]{1,0:T(8,128)(2,1)} async-done(((bf16[1024,704]{1,0:T(8,128)(2,1)}), bf16[128,704]{1,0:T(8,128)(2,1)}) %reduce-scatter.58.cloned.1.call-update) | async-done | bytes 180240
  1470.5 31.6 %reduce-scatter.34.cloned.1.call-done = bf16[256,1024]{1,0:T(8,128)(2,1)} async-done(((bf16[1024,1024]{1,0:T(8,128)(2,1)}), bf16[256,1024]{1,0:T(8,128)(2,1)}) %reduce-scatter.34.cloned.1.call-update) | async-done | bytes 524304 | tf_op jit(solution)/shard_map/reduce_scatter | solution.py:285
  1514.2 21.9 %reduce-scatter.32.cloned.1.call-done = bf16[256,1024]{1,0:T(8,128)(2,1)} async-done(((bf16[1024,1024]{1,0:T(8,128)(2,1)}), bf16[256,1024]{1,0:T(8,128)(2,1)}) %reduce-scatter.32.cloned.1.call-update) | async-done | bytes 524304 | tf_op jit(solution)/shard_map/reduce_scatter | solution.py:282
  1544.2 39.7 %all-reduce = (f32[1024]{0:T(1024)}, f32[1024]{0:T(1024)}, f32[]{:T(128)}, f32[]{:T(128)}) all-reduce(f32[1024]{0:T(1024)S(1)} %get-tuple-element.384, f32[1024]{0:T(1024)S(1)} %copy-done.32, f32[]{:T(128)} %fusion.47, f32[]{:T(128)} %get-tuple-element.459), channel_id=1, replica_groups=mesh['dp'=4,'blk'=8] {'dp','blk'}, use_global_device_ids=true, to_apply=%region_30.31 | all-reduce | flops 2050 | bytes 16400 | tf_op jit(solution)/shard_map/psum | solution.py:327
  1590.9 10.4 reduce-scatter.50.cloned.1.call-done
  1602.9 62.8 %reduce-scatter.48.cloned.1.call-done = bf16[128,256]{1,0:T(8,128)(2,1)} async-done(((bf16[1024,256]{1,0:T(8,128)(2,1)}), bf16[128,256]{1,0:T(8,128)(2,1)}) %reduce-scatter.48.cloned.1.call-update) | async-done | bytes 65552
  1667.3 62.6 %reduce-scatter.46.cloned.1.call-done = bf16[128,256]{1,0:T(8,128)(2,1)} async-done(((bf16[1024,256]{1,0:T(8,128)(2,1)}), bf16[128,256]{1,0:T(8,128)(2,1)}) %reduce-scatter.46.cloned.1.call-update) | async-done | bytes 65552
  (285 shorter events, 277.5 us)
Async XLA Ops:
  7.2 134.5 %all-gather.5.cloned.1.call-start = ((), (), s32[]{:S(2)}) async-start(), calls=%async_computation.16 | async-start | bytes 9437184 | tf_op jit(solution)/shard_map/all_gather | solution.py:147
  9.1 18.2 %copy-start.28 = (f32[256,2]{0,1:T(2,128)}, f32[256,2]{0,1:T(2,128)S(1)}, u32[]{:S(2)}) copy-start(f32[256,2]{0,1:T(2,128)S(1)} %add_rsqrt_fusion.1) | copy-start | bytes 6148
  9.1 4.9 copy-start.31
  13.9 253.7 %all-gather.3.cloned.1.call-start = ((), (), s32[]{:S(2)}) async-start(), calls=%async_computation.15 | async-start | bytes 9437184 | tf_op jit(solution)/shard_map/all_gather | solution.py:146
  18.1 5.8 copy-start.5
  18.1 5.8 copy-start.26
  23.9 4.8 copy-start.23
  23.9 3.4 copy-start.14
  31.8 928.8 %reduce-scatter.30.cloned.1.call-start = ((), (), s32[]{:S(2)}) async-start(), calls=%async_computation.17 | async-start | bytes 18874368 | tf_op jit(solution)/shard_map/reduce_scatter | solution.py:259
  32.4 2.1 copy-start.17
  423.8 2.5 copy-start.11
  426.4 10.2 slice-start.2
  427.8 29.2 %copy-start.3 = (f32[256,2,1024]{2,0,1:T(8,128)}, f32[256,2,1024]{2,0,1:T(8,128)S(1)}, u32[]{:S(2)}) copy-start(f32[256,2,1024]{2,0,1:T(8,128)S(1)} %get-tuple-element.470) | copy-start | bytes 6291460
  428.1 8.4 copy-start.15
  428.1 8.4 slice-start.3
  428.1 18.9 %slice-start = ((s8[5767168]{0:T(1024)(128)(4,1)}), s8[4194304]{0:T(1024)(128)(4,1)S(1)}, s32[]{:S(2)}) async-start(s8[5767168]{0:T(1024)(128)(4,1)} %bitcast.283), calls=%async_computation.32 | async-start | bytes 8388608
  436.6 10.4 slice-start.1
  447.0 6.0 copy-start.33
  453.0 4.0 copy-start.18
  494.2 9.4 copy-start.2
  541.3 9.4 copy-start.2
  589.9 9.4 copy-start.2
  638.4 9.4 copy-start.2
  680.4 313.9 %reduce-scatter.38.cloned.1.call-start = ((), (), s32[]{:S(2)}) async-start(), calls=%async_computation.21 | async-start | bytes 2621440 | tf_op jit(solution)/shard_map/reduce_scatter | solution.py:291
  685.8 365.8 %reduce-scatter.40.cloned.1.call-start = ((), (), s32[]{:S(2)}) async-start(), calls=%async_computation.22 | async-start | bytes 7208960 | tf_op jit(solution)/shard_map/reduce_scatter | solution.py:294
  693.9 415.1 %reduce-scatter.42.cloned.1.call-start = ((), (), s32[]{:S(2)}) async-start(), calls=%async_computation.23 | async-start | bytes 7208960 | tf_op jit(solution)/shard_map/reduce_scatter | solution.py:297
  700.8 465.7 %reduce-scatter.44.cloned.1.call-start = ((), (), s32[]{:S(2)}) async-start(), calls=%async_computation.24 | async-start | bytes 7208960 | tf_op jit(solution)/shard_map/reduce_scatter | solution.py:300
  709.0 255.9 %copy-start.7 = (bf16[256,2,1024]{2,1,0:T(2,128)(2,1)S(1)}, bf16[256,2,1024]{2,1,0:T(2,128)(2,1)}, u32[]{:S(2)}) copy-start(bf16[256,2,1024]{2,1,0:T(2,128)(2,1)} %param.17) | copy-start | bytes 3145732
  709.0 255.9 %copy-start.27 = (f32[1024]{0:T(1024)S(1)}, f32[1024]{0:T(1024)}, u32[]{:S(2)}) copy-start(f32[1024]{0:T(1024)} %param.27) | copy-start | bytes 12292
  709.0 255.9 %copy-start.29 = (f32[256,2]{0,1:T(2,128)S(1)}, f32[256,2]{0,1:T(2,128)}, u32[]{:S(2)}) copy-start(f32[256,2]{0,1:T(2,128)} %copy-done.28) | copy-start | bytes 6148
  709.0 491.7 %reduce-scatter.36.cloned.1.call-start = ((), (), s32[]{:S(2)}) async-start(), calls=%async_computation.20 | async-start | bytes 2621440 | tf_op jit(solution)/shard_map/reduce_scatter | solution.py:288
  962.8 2.1 copy-start.4
  967.8 298.1 %reduce-scatter.52.cloned.1.call-start = ((), (), s32[]{:S(2)}) async-start(), calls=%async_computation.28 | async-start | bytes 589824
  996.3 337.2 %reduce-scatter.54.cloned.1.call-start = ((), (), s32[]{:S(2)}) async-start(), calls=%async_computation.29 | async-start | bytes 1622016
  1054.2 347.0 %reduce-scatter.56.cloned.1.call-start = ((), (), s32[]{:S(2)}) async-start(), calls=%async_computation.30 | async-start | bytes 1622016
  1111.6 357.0 %reduce-scatter.58.cloned.1.call-start = ((), (), s32[]{:S(2)}) async-start(), calls=%async_computation.31 | async-start | bytes 1769472
  1169.1 333.0 %reduce-scatter.34.cloned.1.call-start = ((), (), s32[]{:S(2)}) async-start(), calls=%async_computation.19 | async-start | bytes 2621440 | tf_op jit(solution)/shard_map/reduce_scatter | solution.py:285
  1171.9 3.0 copy-start.24
  1171.9 3.0 copy-start.25
  1183.1 353.0 %reduce-scatter.32.cloned.1.call-start = ((), (), s32[]{:S(2)}) async-start(), calls=%async_computation.18 | async-start | bytes 2621440 | tf_op jit(solution)/shard_map/reduce_scatter | solution.py:282
  1187.4 413.8 %reduce-scatter.50.cloned.1.call-start = ((), (), s32[]{:S(2)}) async-start(), calls=%async_computation.27 | async-start | bytes 589824
  1202.7 463.0 %reduce-scatter.48.cloned.1.call-start = ((), (), s32[]{:S(2)}) async-start(), calls=%async_computation.26 | async-start | bytes 589824
  1504.1 225.8 %reduce-scatter.46.cloned.1.call-start = ((), (), s32[]{:S(2)}) async-start(), calls=%async_computation.25 | async-start | bytes 589824
  1506.0 3.0 copy-start.12
  1506.0 3.0 copy-start.22
  1508.9 2.7 copy-start.13
  1508.9 2.7 copy-start.20
  1538.2 6.0 copy-start.32
  (13 other events, 18.7 us)
Sparse Core Ops, SparseCore 0:
  14.1 127.5 all-gather.4
  144.5 123.0 all-gather.2
  680.5 280.1 reduce-scatter.29
  963.8 30.4 reduce-scatter.37
  996.7 54.8 reduce-scatter.39
  1054.1 54.8 reduce-scatter.41
  1111.6 54.8 reduce-scatter.43
  1169.2 31.4 reduce-scatter.35
  1204.0 61.8 reduce-scatter.51
  1269.6 63.9 reduce-scatter.53
  1337.4 63.8 reduce-scatter.55
  1404.9 63.6 reduce-scatter.57
  1471.7 30.3 reduce-scatter.33
  1504.6 31.4 reduce-scatter.31
  1539.3 61.9 reduce-scatter.49
  1604.8 60.8 reduce-scatter.47
  1668.9 60.9 reduce-scatter.45
where the time goes:
time: 1750 us; the launch traced here: 1740 us
  waiting for transfers between devices  1110 us (63%)
  matrix products  317 us (18%)
  local copies, waits for them, and re-layouts  150 us (9%)
  other arithmetic  89.3 us (5%)
  blocking collectives  39.7 us (2%)
  between operations  18.2 us (1%)
    unnamed x24, waiting for transfers between devices  385 us
    reduce_scatter x1, waiting for transfers between devices, body(): lax.psum_scatter(terms.astype(jnp.bfloat16), 'blk', scatter_dimension=0,...  252 us
    all_gather x1, waiting for transfers between devices, body(): key_piece = lax.all_gather(keys_rot, 'blk', axis=0, tiled=True)  114 us
    all_gather x1, waiting for transfers between devices, body(): value_piece = lax.all_gather(mixed_low, 'blk', axis=0, tiled=True)  99.5 us
    unnamed x95, local copies, waits for them, and re-layouts  72 us
    reduce_scatter x1, waiting for transfers between devices, body(): lax.psum_scatter(weight_grads[4].astype(jnp.bfloat16), 'dp', scatter_dime...  55.2 us
    reduce_scatter x1, waiting for transfers between devices, body(): lax.psum_scatter(weight_grads[6].astype(jnp.bfloat16), 'dp', scatter_dime...  54.8 us
    reduce_scatter x1, waiting for transfers between devices, body(): lax.psum_scatter(weight_grads[5].astype(jnp.bfloat16), 'dp', scatter_dime...  54.8 us
  transfers between devices with their start and end apart: 17, of which 17 were waited for; matrix products, arithmetic and copies ran while one was open for 8% of the time, Pallas kernels for 0%

commit v1 on v0

--- a/solution.py
+++ b/solution.py
@@ -6,6 +6,12 @@
 HEADS = 16
 HEAD_DIM = 64
 epsilon = 1e-06
+
+
+def joined_along(pieces, dim):
+    pieces = jnp.moveaxis(pieces, 0, dim)
+    shape = pieces.shape
+    return pieces.reshape(*shape[:dim], shape[dim] * shape[dim + 1], *shape[dim + 2 :])
 
 
 def documents(doc_lengths, row_length):
@@ -144,7 +150,19 @@
     )
     running = start_state
     key_piece = lax.all_gather(keys_rot, "blk", axis=0, tiled=True)
-    value_piece = lax.all_gather(mixed_low, "blk", axis=0, tiled=True)
+    devices = lax.axis_size("blk")
+    pairs = [(i, (i + 1) % devices) for i in range(devices)]
+    back = [(b, a) for a, b in pairs]
+    lower, upper = ([], [])
+    for step in range(devices - 1):
+        if step % 2 == 0:
+            lower.append(lax.ppermute(lower[-1] if lower else mixed_low, "blk", pairs))
+        else:
+            upper.append(lax.ppermute(upper[-1] if upper else mixed_low, "blk", back))
+    blocks = jnp.stack([*lower[::-1], mixed_low, *upper])
+    shift = lax.axis_index("blk") - len(lower)
+    blocks = blocks[(jnp.arange(devices) - shift) % devices]
+    value_piece = joined_along(blocks, 0)
     n_keys = key_piece.shape[0]
     step_rows = min(512, n_keys)
     n_steps = n_keys // step_rows

time: 1750 us -> 1840 us (1.051)
  starting transfers between devices: 1.81 us -> 81.8 us
  local copies, waits for them, and re-layouts: 150 us -> 211 us
  waiting for transfers between devices: 1110 us -> 1050 us
    ppermute x0 -> x7, waiting for transfers between devices: none -> 139 us  [the longest x4 139 us: body(): lower.append(lax.ppermute(lower[-1] if lower else mixed_low, 'blk', pairs))]
    all_gather x1, waiting for transfers between devices: 114 us -> 0.01 us  [body(): key_piece = lax.all_gather(keys_rot, 'blk', axis=0, tiled=True)]
    all_gather x1, waiting for transfers between devices: 99.5 us -> 0.02 us  [body(): lax.all_gather(mixed_low, 'blk', axis=0, tiled=True)]
    ppermute x0 -> x7, starting transfers between devices: none -> 80.9 us  [the longest x3 72.8 us: body(): upper.append(lax.ppermute(upper[-1] if upper else mixed_low, 'blk', back))]
    dynamic_slice x16 -> x32, local copies, waits for them, and re-layouts: 35.2 us -> 74.7 us  [body(): lax.scan(inner_step, running, (key_piece.reshape(n_steps, step_rows, seq_...]
    unnamed x95 -> x109, local copies, waits for them, and re-layouts: 72 us -> 74.2 us
  transfers between devices with their start and end apart: 17 -> 24, of which waited for: 17 -> 19; matrix products, arithmetic and copies ran while one was open for 8% -> 20% of each run, Pallas kernels for 0% -> 0%
where the time goes in v1:
time: 1840 us; the launch traced here: 1830 us
  waiting for transfers between devices  1050 us (57%)
  matrix products  320 us (17%)
  local copies, waits for them, and re-layouts  211 us (11%)
  other arithmetic  93.8 us (5%)
  starting transfers between devices  81.8 us (4%)
  blocking collectives  39.8 us (2%)
    unnamed x24, waiting for transfers between devices  385 us
    reduce_scatter x1, waiting for transfers between devices, body(): lax.psum_scatter(terms.astype(jnp.bfloat16), 'blk', scatter_dimension=0,...  265 us
    ppermute x4, waiting for transfers between devices, body(): lower.append(lax.ppermute(lower[-1] if lower else mixed_low, 'blk', pairs))  139 us
    dynamic_slice x32, local copies, waits for them, and re-layouts, body(): lax.scan(inner_step, running, (key_piece.reshape(n_steps, step_rows, seq_...  74.7 us
    unnamed x109, local copies, waits for them, and re-layouts  74.2 us
    ppermute x3, starting transfers between devices, body(): upper.append(lax.ppermute(upper[-1] if upper else mixed_low, 'blk', back))  72.8 us
    reduce_scatter x1, waiting for transfers between devices, body(): lax.psum_scatter(weight_grads[4].astype(jnp.bfloat16), 'dp', scatter_dime...  55.1 us
    reduce_scatter x1, waiting for transfers between devices, body(): lax.psum_scatter(weight_grads[5].astype(jnp.bfloat16), 'dp', scatter_dime...  54.9 us
  transfers between devices with their start and end apart: 24, of which 19 were waited for; matrix products, arithmetic and copies ran while one was open for 20% of the time, Pallas kernels for 0%

profile of v1, /device:TPU:0, one launch (start us, length us, event | category | flops | bytes accessed | tf_op | source)
XLA Modules:
  0.0 1827.9 jit_solution(6879398368892517255)
XLA Ops:
  42.1 43.8 %collective-permute-done = bf16[256,2,1024]{2,0,1:T(8,128)(2,1)S(1)} collective-permute-done((bf16[256,2,1024]{2,0,1:T(8,128)(2,1)}, bf16[256,2,1024]{2,0,1:T(8,128)(2,1)S(1)}, u32[]{:S(2)}, u32[]{:S(2)}) %collective-permute-start) | collective-permute-done | bytes 1048608 | tf_op jit(solution)/shard_map/ppermute | solution.py:159
  91.7 55.0 %collective-permute-done.1 = bf16[256,2,1024]{2,0,1:T(8,128)(2,1)S(1)} collective-permute-done((bf16[256,2,1024]{2,0,1:T(8,128)(2,1)S(1)}, bf16[256,2,1024]{2,0,1:T(8,128)(2,1)S(1)}, u32[]{:S(2)}, u32[]{:S(2)}) %collective-permute-start.1) | collective-permute-done | bytes 1048608 | tf_op jit(solution)/shard_map/ppermute | solution.py:159
  150.0 45.4 %collective-permute-start.5 = (bf16[256,2,1024]{2,0,1:T(8,128)(2,1)}, bf16[256,2,1024]{2,0,1:T(8,128)(2,1)}, u32[]{:S(2)}, u32[]{:S(2)}) collective-permute-start(bf16[256,2,1024]{2,0,1:T(8,128)(2,1)} %collective-permute-done.4), channel_id=1, source_target_pairs={{1,0},{2,1},{3,2},{4,3},{5,4},{6,5},{7,6},{0,7},{9,8},{10,9},{11,1... | collective-permute-start | bytes 3145736 | tf_op jit(solution)/shard_map/ppermute | solution.py:161
  195.4 21.3 %collective-permute-done.2 = bf16[256,2,1024]{2,0,1:T(8,128)(2,1)} collective-permute-done((bf16[256,2,1024]{2,0,1:T(8,128)(2,1)S(1)}, bf16[256,2,1024]{2,0,1:T(8,128)(2,1)}, u32[]{:S(2)}, u32[]{:S(2)}) %collective-permute-start.2) | collective-permute-done | bytes 1048608 | tf_op jit(solution)/shard_map/ppermute | solution.py:159
  228.8 22.7 %collective-permute-start.6 = (bf16[256,2,1024]{2,0,1:T(8,128)(2,1)}, bf16[256,2,1024]{2,0,1:T(8,128)(2,1)S(1)}, u32[]{:S(2)}, u32[]{:S(2)}) collective-permute-start(bf16[256,2,1024]{2,0,1:T(8,128)(2,1)} %collective-permute-done.5), channel_id=1, source_target_pairs={{1,0},{2,1},{3,2},{4,3},{5,4},{6,5},{7,6},{0,7},{9,8},{10,9},{11,1... | collective-permute-start | bytes 3145736 | tf_op jit(solution)/shard_map/ppermute | solution.py:161
  251.5 19.0 %collective-permute-done.3 = bf16[256,2,1024]{2,0,1:T(8,128)(2,1)} collective-permute-done((bf16[256,2,1024]{2,0,1:T(8,128)(2,1)}, bf16[256,2,1024]{2,0,1:T(8,128)(2,1)}, u32[]{:S(2)}, u32[]{:S(2)}) %collective-permute-start.3) | collective-permute-done | bytes 1048608 | tf_op jit(solution)/shard_map/ppermute | solution.py:159
  300.1 11.6 copy.141
  311.7 165.6 %while.28 = (s32[]{:T(128)}, f32[2,16,256]{2,1,0:T(8,128)S(1)}, f32[2,16,256]{2,1,0:T(8,128)S(1)}, f32[2,16,256,64]{2,3,1,0:T(8,128)}, s32[4]{0:T(128)S(1)}, /*i...) while((s32[]{:T(128)}, f32[2,16,256]{2,1,0:T(8,128)S(1)}, ...), condition=%wide.region_7.8_spmd.clone, body=%wide.region_4.0_spmd.clone.sunk | while | flops 1122149120 | bytes 74207448 | solution.py:174
  332.2 9.2 fusion.161
  341.4 11.9 fusion.163
  373.8 9.2 fusion.161
  383.0 11.7 fusion.163
  415.1 9.2 fusion.161
  424.3 11.7 fusion.163
  456.3 9.2 fusion.161
  465.5 11.7 fusion.163
  481.6 8.4 fusion.35
  490.1 10.2 multiply_convert_fusion.1
  519.2 212.7 %while.29 = (s32[]{:T(128)}, f32[256,2,16,64]{0,3,2,1:T(8,128)}, bf16[4,512,2,2048]{1,3,2,0:T(8,128)(2,1)}, bf16[4,512,2,1024]{1,3,2,0:T(8,128)(2,1)}, s32[4]{0:...) while((s32[]{:T(128)}, f32[256,2,16,64]{0,3,2,1:T(8,128)}, ...), condition=%wide.region_12.13_spmd.clone, body=%wide.region_11.12_spmd.clone.sunk | while | flops 2739012352 | bytes 133288232 | solution.py:267
  533.9 8.1 fusion.174
  542.0 10.6 fusion.176
  552.6 9.4 fusion.175
  585.8 8.1 fusion.174
  593.9 10.6 fusion.176
  604.6 9.4 fusion.175
  639.4 8.1 fusion.174
  647.5 10.6 fusion.176
  658.1 9.4 fusion.175
  692.9 8.1 fusion.174
  701.0 10.6 fusion.176
  711.7 9.4 fusion.175
  732.0 22.1 %copy.150 = bf16[4,512,2,2048]{3,1,0,2:T(8,128)(2,1)} copy(bf16[4,512,2,2048]{1,3,2,0:T(8,128)(2,1)} %get-tuple-element.145) | data formatting | bytes 33554432 | tf_op jit(solution)/shard_map/convert_element_type | solution.py:278
  782.6 265.4 %reduce-scatter.30.cloned.1.call-done = bf16[256,2,2048]{2,0,1:T(8,128)(2,1)} async-done(((bf16[2048,2,2048]{2,0,1:T(8,128)(2,1)}), bf16[256,2,2048]{2,0,1:T(8,128)(2,1)}) %reduce-scatter.30.cloned.1.call-update) | async-done | bytes 2097168 | tf_op jit(solution)/shard_map/reduce_scatter | solution.py:277
  1055.2 26.4 %reduce-scatter.38.cloned.1.call-done = bf16[256,1024]{1,0:T(8,128)(2,1)} async-done(((bf16[1024,1024]{1,0:T(8,128)(2,1)}), bf16[256,1024]{1,0:T(8,128)(2,1)}) %reduce-scatter.38.cloned.1.call-update) | async-done | bytes 524304 | tf_op jit(solution)/shard_map/reduce_scatter | solution.py:309
  1083.7 55.1 %reduce-scatter.40.cloned.1.call-done = bf16[256,2816]{1,0:T(8,128)(2,1)} async-done(((bf16[1024,2816]{1,0:T(8,128)(2,1)}), bf16[256,2816]{1,0:T(8,128)(2,1)}) %reduce-scatter.40.cloned.1.call-update) | async-done | bytes 1441808 | tf_op jit(solution)/shard_map/reduce_scatter | solution.py:312
  1141.5 54.9 %reduce-scatter.42.cloned.1.call-done = bf16[256,2816]{1,0:T(8,128)(2,1)} async-done(((bf16[1024,2816]{1,0:T(8,128)(2,1)}), bf16[256,2816]{1,0:T(8,128)(2,1)}) %reduce-scatter.42.cloned.1.call-update) | async-done | bytes 1441808 | tf_op jit(solution)/shard_map/reduce_scatter | solution.py:315
  1199.0 54.8 %reduce-scatter.44.cloned.1.call-done = bf16[704,1024]{1,0:T(8,128)(2,1)} async-done(((bf16[2816,1024]{1,0:T(8,128)(2,1)}), bf16[704,1024]{1,0:T(8,128)(2,1)}) %reduce-scatter.44.cloned.1.call-update) | async-done | bytes 1441808 | tf_op jit(solution)/shard_map/reduce_scatter | solution.py:318
  1274.8 13.2 reduce-scatter.36.cloned.1.call-done
  1301.7 51.5 %reduce-scatter.52.cloned.1.call-done = bf16[128,256]{1,0:T(8,128)(2,1)} async-done(((bf16[1024,256]{1,0:T(8,128)(2,1)}), bf16[128,256]{1,0:T(8,128)(2,1)}) %reduce-scatter.52.cloned.1.call-update) | async-done | bytes 65552
  1354.9 66.0 %reduce-scatter.54.cloned.1.call-done = bf16[352,256]{1,0:T(8,128)(2,1)} async-done(((bf16[2816,256]{1,0:T(8,128)(2,1)}), bf16[352,256]{1,0:T(8,128)(2,1)}) %reduce-scatter.54.cloned.1.call-update) | async-done | bytes 180240
  1422.8 65.8 %reduce-scatter.56.cloned.1.call-done = bf16[352,256]{1,0:T(8,128)(2,1)} async-done(((bf16[2816,256]{1,0:T(8,128)(2,1)}), bf16[352,256]{1,0:T(8,128)(2,1)}) %reduce-scatter.56.cloned.1.call-update) | async-done | bytes 180240
  1490.6 65.4 %reduce-scatter.58.cloned.1.call-done = bf16[128,704]{1,0:T(8,128)(2,1)} async-done(((bf16[1024,704]{1,0:T(8,128)(2,1)}), bf16[128,704]{1,0:T(8,128)(2,1)}) %reduce-scatter.58.cloned.1.call-update) | async-done | bytes 180240
  1557.8 31.6 %reduce-scatter.34.cloned.1.call-done = bf16[256,1024]{1,0:T(8,128)(2,1)} async-done(((bf16[1024,1024]{1,0:T(8,128)(2,1)}), bf16[256,1024]{1,0:T(8,128)(2,1)}) %reduce-scatter.34.cloned.1.call-update) | async-done | bytes 524304 | tf_op jit(solution)/shard_map/reduce_scatter | solution.py:303
  1601.8 21.6 %reduce-scatter.32.cloned.1.call-done = bf16[256,1024]{1,0:T(8,128)(2,1)} async-done(((bf16[1024,1024]{1,0:T(8,128)(2,1)}), bf16[256,1024]{1,0:T(8,128)(2,1)}) %reduce-scatter.32.cloned.1.call-update) | async-done | bytes 524304 | tf_op jit(solution)/shard_map/reduce_scatter | solution.py:300
  1631.5 39.8 %all-reduce = (f32[1024]{0:T(1024)}, f32[1024]{0:T(1024)}, f32[]{:T(128)}, f32[]{:T(128)}) all-reduce(f32[1024]{0:T(1024)S(1)} %get-tuple-element.373, f32[1024]{0:T(1024)S(1)} %copy-done.36, f32[]{:T(128)} %fusion.47, f32[]{:T(128)} %get-tuple-element.444), channel_id=1, replica_groups=mesh['dp'=4,'blk'=8] {'dp','blk'}, use_global_device_ids=true, to_apply=%region_30.31 | all-reduce | flops 2050 | bytes 16400 | tf_op jit(solution)/shard_map/psum | solution.py:345
  1678.3 10.3 reduce-scatter.50.cloned.1.call-done
  1690.2 62.9 %reduce-scatter.48.cloned.1.call-done = bf16[128,256]{1,0:T(8,128)(2,1)} async-done(((bf16[1024,256]{1,0:T(8,128)(2,1)}), bf16[128,256]{1,0:T(8,128)(2,1)}) %reduce-scatter.48.cloned.1.call-update) | async-done | bytes 65552
  1754.7 62.5 %reduce-scatter.46.cloned.1.call-done = bf16[128,256]{1,0:T(8,128)(2,1)} async-done(((bf16[1024,256]{1,0:T(8,128)(2,1)}), bf16[128,256]{1,0:T(8,128)(2,1)}) %reduce-scatter.46.cloned.1.call-update) | async-done | bytes 65552
  (334 shorter events, 390.1 us)
Async XLA Ops:
  7.2 27.5 %copy-start = (bf16[1024,1024]{1,0:T(8,128)(2,1)S(1)}, bf16[1024,1024]{1,0:T(8,128)(2,1)}, u32[]{:S(2)}) copy-start(bf16[1024,1024]{1,0:T(8,128)(2,1)} %param.22) | copy-start | bytes 6291460
  7.2 292.9 %all-gather.3.cloned.1.call-start = ((), (), s32[]{:S(2)}) async-start(), calls=%async_computation.15 | async-start | bytes 9437184 | tf_op jit(solution)/shard_map/all_gather | solution.py:152
  9.8 24.8 %copy-start.33 = (f32[256,2]{0,1:T(2,128)}, f32[256,2]{0,1:T(2,128)S(1)}, u32[]{:S(2)}) copy-start(f32[256,2]{0,1:T(2,128)S(1)} %add_rsqrt_fusion.1) | copy-start | bytes 6148
  15.2 4.0 copy-start.5
  15.2 4.0 copy-start.31
  19.3 4.4 copy-start.15
  27.4 3.9 copy-start.28
  34.6 484.6 %all-gather.5.cloned.1.call-start = ((), (), s32[]{:S(2)}) async-start(), calls=%async_computation.16 | async-start | bytes 9437184 | tf_op jit(solution)/shard_map/all_gather | solution.py:219
  39.1 46.8 %collective-permute-start = (bf16[256,2,1024]{2,0,1:T(8,128)(2,1)}, bf16[256,2,1024]{2,0,1:T(8,128)(2,1)S(1)}, u32[]{:S(2)}, u32[]{:S(2)}) collective-permute-start(bf16[256,2,1024]{2,0,1:T(8,128)(2,1)} %get-tuple-element.445), channel_id=1, source_target_pairs={{0,1},{1,2},{2,3},{3,4},{4,5},{5,6},{6,7},{7,0},{8,9},{9,10},{10,1... | collective-permute-start | bytes 3145736 | tf_op jit(solution)/shard_map/ppermute | solution.py:159
  86.9 59.8 %collective-permute-start.1 = (bf16[256,2,1024]{2,0,1:T(8,128)(2,1)S(1)}, bf16[256,2,1024]{2,0,1:T(8,128)(2,1)S(1)}, u32[]{:S(2)}, u32[]{:S(2)}) collective-permute-start(bf16[256,2,1024]{2,0,1:T(8,128)(2,1)S(1)} %collective-permute-done), channel_id=1, source_target_pairs={{0,1},{1,2},{2,3},{3,4},{4,5},{5,6},{6,7},{7,0},{8,9},{9,10},{10,1... | collective-permute-start | bytes 3145736 | tf_op jit(solution)/shard_map/ppermute | solution.py:159
  86.9 63.0 %collective-permute-start.4 = (bf16[256,2,1024]{2,0,1:T(8,128)(2,1)}, bf16[256,2,1024]{2,0,1:T(8,128)(2,1)}, u32[]{:S(2)}, u32[]{:S(2)}) collective-permute-start(bf16[256,2,1024]{2,0,1:T(8,128)(2,1)} %get-tuple-element.445), channel_id=1, source_target_pairs={{1,0},{2,1},{3,2},{4,3},{5,4},{6,5},{7,6},{0,7},{9,8},{10,9},{11,1... | collective-permute-start | bytes 3145736 | tf_op jit(solution)/shard_map/ppermute | solution.py:161
  146.7 72.6 %copy-start.20 = (bf16[256,2,1024]{2,0,1:T(8,128)(2,1)}, bf16[256,2,1024]{2,0,1:T(8,128)(2,1)S(1)}, u32[]{:S(2)}) copy-start(bf16[256,2,1024]{2,0,1:T(8,128)(2,1)S(1)} %collective-permute-done.1) | copy-start | bytes 3145732
  146.7 69.9 %collective-permute-start.2 = (bf16[256,2,1024]{2,0,1:T(8,128)(2,1)S(1)}, bf16[256,2,1024]{2,0,1:T(8,128)(2,1)}, u32[]{:S(2)}, u32[]{:S(2)}) collective-permute-start(bf16[256,2,1024]{2,0,1:T(8,128)(2,1)S(1)} %collective-permute-done.1), channel_id=1, source_target_pairs={{0,1},{1,2},{2,3},{3,4},{4,5},{5,6},{6,7},{7,0},{8,9},{9,10},{10,1... | collective-permute-start | bytes 3145736 | tf_op jit(solution)/shard_map/ppermute | solution.py:159
  149.2 898.8 %reduce-scatter.30.cloned.1.call-start = ((), (), s32[]{:S(2)}) async-start(), calls=%async_computation.17 | async-start | bytes 18874368 | tf_op jit(solution)/shard_map/reduce_scatter | solution.py:277
  150.0 78.8 %collective-permute-start.5 = (bf16[256,2,1024]{2,0,1:T(8,128)(2,1)}, bf16[256,2,1024]{2,0,1:T(8,128)(2,1)}, u32[]{:S(2)}, u32[]{:S(2)}) collective-permute-start(bf16[256,2,1024]{2,0,1:T(8,128)(2,1)} %collective-permute-done.4), channel_id=1, source_target_pairs={{1,0},{2,1},{3,2},{4,3},{5,4},{6,5},{7,6},{0,7},{9,8},{10,9},{11,1... | collective-permute-start | bytes 3145736 | tf_op jit(solution)/shard_map/ppermute | solution.py:161
  216.6 53.9 %collective-permute-start.3 = (bf16[256,2,1024]{2,0,1:T(8,128)(2,1)}, bf16[256,2,1024]{2,0,1:T(8,128)(2,1)}, u32[]{:S(2)}, u32[]{:S(2)}) collective-permute-start(bf16[256,2,1024]{2,0,1:T(8,128)(2,1)} %collective-permute-done.2), channel_id=1, source_target_pairs={{0,1},{1,2},{2,3},{3,4},{4,5},{5,6},{6,7},{7,0},{8,9},{9,10},{10,1... | collective-permute-start | bytes 3145736 | tf_op jit(solution)/shard_map/ppermute | solution.py:159
  228.8 46.5 %copy-start.21 = (bf16[256,2,1024]{2,0,1:T(8,128)(2,1)S(1)}, bf16[256,2,1024]{2,0,1:T(8,128)(2,1)}, u32[]{:S(2)}) copy-start(bf16[256,2,1024]{2,0,1:T(8,128)(2,1)} %copy-done.20) | copy-start | bytes 3145732
  228.8 54.2 %collective-permute-start.6 = (bf16[256,2,1024]{2,0,1:T(8,128)(2,1)}, bf16[256,2,1024]{2,0,1:T(8,128)(2,1)S(1)}, u32[]{:S(2)}, u32[]{:S(2)}) collective-permute-start(bf16[256,2,1024]{2,0,1:T(8,128)(2,1)} %collective-permute-done.5), channel_id=1, source_target_pairs={{1,0},{2,1},{3,2},{4,3},{5,4},{6,5},{7,6},{0,7},{9,8},{10,9},{11,1... | collective-permute-start | bytes 3145736 | tf_op jit(solution)/shard_map/ppermute | solution.py:161
  479.9 10.2 slice-start.2
  481.3 29.1 %copy-start.3 = (f32[256,2,1024]{2,0,1:T(8,128)}, f32[256,2,1024]{2,0,1:T(8,128)S(1)}, u32[]{:S(2)}) copy-start(f32[256,2,1024]{2,0,1:T(8,128)S(1)} %get-tuple-element.455) | copy-start | bytes 6291460
  481.6 8.5 copy-start.16
  481.6 8.5 slice-start.3
  481.6 18.7 %slice-start = ((s8[5767168]{0:T(1024)(128)(4,1)}), s8[4194304]{0:T(1024)(128)(4,1)S(1)}, s32[]{:S(2)}) async-start(s8[5767168]{0:T(1024)(128)(4,1)} %bitcast.303), calls=%async_computation.32 | async-start | bytes 8388608
  490.1 10.3 slice-start.1
  500.3 6.0 copy-start.37
  506.4 4.0 copy-start.23
  552.6 9.4 copy-start.2
  604.6 9.4 copy-start.2
  658.1 9.4 copy-start.2
  711.7 9.4 copy-start.2
  754.1 327.5 %reduce-scatter.38.cloned.1.call-start = ((), (), s32[]{:S(2)}) async-start(), calls=%async_computation.21 | async-start | bytes 2621440 | tf_op jit(solution)/shard_map/reduce_scatter | solution.py:309
  759.5 379.4 %reduce-scatter.40.cloned.1.call-start = ((), (), s32[]{:S(2)}) async-start(), calls=%async_computation.22 | async-start | bytes 7208960 | tf_op jit(solution)/shard_map/reduce_scatter | solution.py:312
  767.5 428.9 %reduce-scatter.42.cloned.1.call-start = ((), (), s32[]{:S(2)}) async-start(), calls=%async_computation.23 | async-start | bytes 7208960 | tf_op jit(solution)/shard_map/reduce_scatter | solution.py:315
  774.3 479.5 %reduce-scatter.44.cloned.1.call-start = ((), (), s32[]{:S(2)}) async-start(), calls=%async_computation.24 | async-start | bytes 7208960 | tf_op jit(solution)/shard_map/reduce_scatter | solution.py:318
  782.5 269.6 %copy-start.7 = (bf16[256,2,1024]{2,1,0:T(2,128)(2,1)S(1)}, bf16[256,2,1024]{2,1,0:T(2,128)(2,1)}, u32[]{:S(2)}) copy-start(bf16[256,2,1024]{2,1,0:T(2,128)(2,1)} %param.17) | copy-start | bytes 3145732
  782.5 269.6 %copy-start.32 = (f32[1024]{0:T(1024)S(1)}, f32[1024]{0:T(1024)}, u32[]{:S(2)}) copy-start(f32[1024]{0:T(1024)} %param.27) | copy-start | bytes 12292
  782.5 269.5 %copy-start.34 = (f32[256,2]{0,1:T(2,128)S(1)}, f32[256,2]{0,1:T(2,128)}, u32[]{:S(2)}) copy-start(f32[256,2]{0,1:T(2,128)} %copy-done.33) | copy-start | bytes 6148
  782.5 505.4 %reduce-scatter.36.cloned.1.call-start = ((), (), s32[]{:S(2)}) async-start(), calls=%async_computation.20 | async-start | bytes 2621440 | tf_op jit(solution)/shard_map/reduce_scatter | solution.py:306
  1055.1 298.1 %reduce-scatter.52.cloned.1.call-start = ((), (), s32[]{:S(2)}) async-start(), calls=%async_computation.28 | async-start | bytes 589824
  1083.7 337.2 %reduce-scatter.54.cloned.1.call-start = ((), (), s32[]{:S(2)}) async-start(), calls=%async_computation.29 | async-start | bytes 1622016
  1141.5 347.2 %reduce-scatter.56.cloned.1.call-start = ((), (), s32[]{:S(2)}) async-start(), calls=%async_computation.30 | async-start | bytes 1622016
  1198.9 357.1 %reduce-scatter.58.cloned.1.call-start = ((), (), s32[]{:S(2)}) async-start(), calls=%async_computation.31 | async-start | bytes 1769472
  1256.4 333.0 %reduce-scatter.34.cloned.1.call-start = ((), (), s32[]{:S(2)}) async-start(), calls=%async_computation.19 | async-start | bytes 2621440 | tf_op jit(solution)/shard_map/reduce_scatter | solution.py:303
  1270.6 352.8 %reduce-scatter.32.cloned.1.call-start = ((), (), s32[]{:S(2)}) async-start(), calls=%async_computation.18 | async-start | bytes 2621440 | tf_op jit(solution)/shard_map/reduce_scatter | solution.py:300
  1274.7 413.9 %reduce-scatter.50.cloned.1.call-start = ((), (), s32[]{:S(2)}) async-start(), calls=%async_computation.27 | async-start | bytes 589824
  1290.0 463.1 %reduce-scatter.48.cloned.1.call-start = ((), (), s32[]{:S(2)}) async-start(), calls=%async_computation.26 | async-start | bytes 589824
  1591.5 225.7 %reduce-scatter.46.cloned.1.call-start = ((), (), s32[]{:S(2)}) async-start(), calls=%async_computation.25 | async-start | bytes 589824
  1625.5 6.0 copy-start.36
  (24 other events, 46.8 us)
Sparse Core Ops, SparseCore 0:
  34.8 239.4 all-gather.2
  277.1 143.0 all-gather.4
  754.2 293.7 reduce-scatter.29
  1051.1 30.4 reduce-scatter.37
  1084.0 54.8 reduce-scatter.39
  1141.4 54.8 reduce-scatter.41
  1198.9 54.8 reduce-scatter.43
  1256.5 31.3 reduce-scatter.35
  1291.3 61.8 reduce-scatter.51
  1356.9 63.9 reduce-scatter.53
  1424.6 63.9 reduce-scatter.55
  1492.3 63.6 reduce-scatter.57
  1559.1 30.2 reduce-scatter.33
  1591.9 31.4 reduce-scatter.31
  1626.6 61.9 reduce-scatter.49
  1692.2 60.8 reduce-scatter.47
  1756.3 60.8 reduce-scatter.45
